TPU v7x, 32 devices: a whole 2x2x4 slice. The times are simulated.
32 devices in a mesh: dp: 2 (over x), tensor: 4 (over z), fsdp: 4 (over y, core).
Axes of the slice: x: 2, y: 2, z: 4, core: 2. Of those that a mesh axis runs over, the one named last changes fastest.
Arguments:
- train_acts: bfloat16 [2048, 4096], P(('dp', 'fsdp'), 'tensor'), may hold values from -6 to 6
- val_acts: bfloat16 [2048, 4096], P(('dp', 'fsdp'), 'tensor'), may hold values from -6 to 6
- train_cot: bfloat16 [2048, 4096], P(('dp', 'fsdp'), 'tensor'), may hold values from -6 to 6
- val_cot: bfloat16 [2048, 4096], P(('dp', 'fsdp'), 'tensor'), may hold values from -6 to 6
- train_lengths: int32 [32], P(('dp', 'fsdp')), may hold values from 16 to 64
- val_lengths: int32 [32], P(('dp', 'fsdp')), may hold values from 16 to 64
- gate_weight: bfloat16 [4096, 11008], P(('dp', 'fsdp'), 'tensor'), may hold values from -0.09375 to 0.09375
- up_weight: bfloat16 [4096, 11008], P(('dp', 'fsdp'), 'tensor'), may hold values from -0.09375 to 0.09375
- in_basis: bfloat16 [11008, 64], P('tensor'), may hold values from -0.0546875 to 0.0546875
- out_basis: bfloat16 [4096, 128], P('tensor'), may hold values from -0.09375 to 0.09375
Outputs:
- scores: float32 [32, 32], P(('dp', 'fsdp'))
Inputs may be any that keep to these rules, and one draw needn't show every extreme that they name: `train_lengths`: an example's first length slots hold its tokens, the rest are padding. `val_lengths`: as for the training examples.
All inputs are finite; a program needn't handle non-finite values.
Results may differ from a plain program's by a relative error of at most 0.004.
Values may be sent and summed in bfloat16 or wider, within the bound.
No kernel may reach another device: no remote copies, remote signals or barrier semaphores. Data moves between devices by JAX's collectives and lax.ppermute only.
A program may use at most 128 MiB of HBM per device.

v0:
```python
import jax
import jax.numpy as jnp
from jax import lax
from jax.sharding import PartitionSpec as P

SEQ = 64


def outer_sums(in_proj, out_proj, valid):
    in_three = in_proj.reshape(valid.shape[0], valid.shape[1], in_proj.shape[1]) * valid[:, :, None]
    out_three = out_proj.reshape(valid.shape[0], valid.shape[1], out_proj.shape[1])
    return jnp.einsum("esj,esk->ejk", in_three, out_three, precision=lax.Precision.HIGHEST)


def on_device(
    train_acts,
    val_acts,
    train_cot,
    val_cot,
    train_lengths,
    val_lengths,
    gate_weight,
    up_weight,
    in_basis,
    out_basis,
):
    train_full, val_full = (
        lax.all_gather(train_acts, "tensor", axis=1, tiled=True),
        lax.all_gather(val_acts, "tensor", axis=1, tiled=True),
    )
    activations = jnp.concatenate([train_full, val_full], axis=0)
    cotangents = jnp.concatenate([train_cot, val_cot], axis=0)
    gate_sum = jnp.dot(
        activations,
        lax.all_gather(gate_weight, ("dp", "fsdp"), axis=0, tiled=True),
        preferred_element_type=jnp.float32,
    )
    up_sum = jnp.dot(
        activations,
        lax.all_gather(up_weight, ("dp", "fsdp"), axis=0, tiled=True),
        preferred_element_type=jnp.float32,
    )
    hidden = (jax.nn.silu(gate_sum) * up_sum).astype(jnp.bfloat16)
    in_part = jnp.dot(hidden, in_basis, preferred_element_type=jnp.float32)
    out_part = jnp.dot(cotangents, out_basis, preferred_element_type=jnp.float32)
    lengths = jnp.concatenate([train_lengths, val_lengths], axis=0)
    valid = (jnp.arange(SEQ, dtype=jnp.int32)[None, :] < lengths[:, None]).astype(jnp.float32)
    in_proj, out_proj = lax.psum((in_part, out_part), "tensor")
    sketch = outer_sums(in_proj, out_proj, valid)
    flat_sketch = sketch.reshape(sketch.shape[0], sketch.shape[1] * sketch.shape[2])
    unit_rows = flat_sketch * lax.rsqrt(
        jnp.sum(flat_sketch * flat_sketch, axis=1, keepdims=True) + 1e-06
    )
    train_count = train_lengths.shape[0]
    train_unit = unit_rows[:train_count]
    val_local = unit_rows[train_count:]
    width_all = flat_sketch.shape[1]
    share = width_all // lax.axis_size("tensor")
    first = lax.axis_index("tensor") * share
    train_share = lax.dynamic_slice_in_dim(train_unit, first, share, 1)
    val_share_local = lax.dynamic_slice_in_dim(val_local, first, share, 1)
    val_share = lax.all_gather(val_share_local, ("dp", "fsdp"), axis=0, tiled=True)
    partial_scores = jnp.dot(
        train_share,
        val_share.T,
        precision=lax.Precision.HIGHEST,
        preferred_element_type=jnp.float32,
    )
    product = lax.psum(partial_scores, "tensor")
    return product * jnp.sqrt(jnp.float32(width_all))


def solution(mesh):
    placed = (
        P(("dp", "fsdp"), "tensor"),
        P(("dp", "fsdp"), "tensor"),
        P(("dp", "fsdp"), "tensor"),
        P(("dp", "fsdp"), "tensor"),
        P(("dp", "fsdp")),
        P(("dp", "fsdp")),
        P(("dp", "fsdp"), "tensor"),
        P(("dp", "fsdp"), "tensor"),
        P("tensor", None),
        P("tensor", None),
    )
    return jax.shard_map(
        on_device, mesh=mesh, in_specs=placed, out_specs=P(("dp", "fsdp"), None), check_vma=False
    )
```

profile of v0, /device:TPU:0, one launch (start us, length us, event | category | flops | bytes accessed | tf_op | source)
XLA Modules:
  0.0 431.9 jit_solution(13203272675145067068)
XLA Ops:
  6.6 0.7 all-gather.6.cloned.1.call-update
  7.3 0.7 all-gather.8.cloned.1.call-update
  8.1 0.7 all-gather.10.cloned.1.call-update
  8.8 0.5 all-gather.12.cloned.1.call-update
  9.4 1.1 fusion.1
  10.6 46.8 %all-gather.6.cloned.1.call-done = bf16[256,4096]{1,0:T(8,128)(2,1)} async-done(((bf16[256,1024]{1,0:T(8,128)(2,1)}), bf16[256,4096]{1,0:T(8,128)(2,1)}) %all-gather.6.cloned.1.call-update) | async-done | bytes 2097168 | tf_op jit(solution)/shard_map/all_gather | solution.py:28
  57.3 3.1 constant_dynamic-update-slice_fusion.1
  60.4 42.9 %all-gather.8.cloned.1.call-done = bf16[256,4096]{1,0:T(8,128)(2,1)} async-done(((bf16[256,1024]{1,0:T(8,128)(2,1)}), bf16[256,4096]{1,0:T(8,128)(2,1)}) %all-gather.8.cloned.1.call-update) | async-done | bytes 2097168 | tf_op jit(solution)/shard_map/all_gather | solution.py:29
  103.4 3.1 constant_dynamic-update-slice_fusion
  106.5 116.1 %all-gather.10.cloned.1.call-done = bf16[4096,2752]{0,1:T(8,128)(2,1)} async-done(((bf16[512,2752]{0,1:T(8,128)(2,1)}), bf16[4096,2752]{0,1:T(8,128)(2,1)}) %all-gather.10.cloned.1.call-update) | async-done | bytes 22544400 | tf_op jit(solution)/shard_map/all_gather | solution.py:35
  222.7 19.2 %fusion.15 = f32[512,2752]{0,1:T(8,128)} fusion(bf16[512,4096]{1,0:T(8,128)(2,1)} %constant_dynamic-update-slice_fusion, bf16[4096,2752]{0,1:T(8,128)(2,1)} %all-gather.10.cloned.1.call-done), kind=kOutput, calls=%fused_computation.25 | convolution fusion | flops 11542724608 | bytes 32374784 | tf_op jit(solution)/shard_map/dot_general | solution.py:33
  241.9 101.1 %all-gather.12.cloned.1.call-done = bf16[4096,2752]{0,1:T(8,128)(2,1)} async-done(((bf16[512,2752]{0,1:T(8,128)(2,1)}), bf16[4096,2752]{0,1:T(8,128)(2,1)}) %all-gather.12.cloned.1.call-update) | async-done | bytes 22544400 | tf_op jit(solution)/shard_map/all_gather | solution.py:40
  343.0 20.0 %fusion = f32[512,64]{0,1:T(8,128)S(1)} fusion(bf16[2752,64]{0,1:T(8,128)(2,1)S(1)} %copy-done, f32[512,2752]{0,1:T(8,128)} %fusion.15, bf16[512,4096]{1,0:T(8,128)(2,1)} %constant_dynamic-update-slice_fusion, bf16[4096,2752]{0,1:T(8,128)(2,1)} %all-gather.12.cloned.1.call-done), kind=kOutput, calls=%fused_computation.1 | convolution fusion | flops 11731533824 | bytes 32858112 | tf_op jit(solution)/shard_map/dot_general | solution.py:44
  363.1 0.1 reshape.37
  363.2 0.8 copy.12
  364.0 0.1 pad_add_fusion
  364.1 38.7 %all-reduce.3.cloned.1.call-done = (f32[8,64,128]{2,1,0:T(8,128)}, f32[8,64,64]{1,2,0:T(8,128)}) async-done(((f32[8,64,128]{2,1,0:T(8,128)}, f32[8,64,64]{1,2,0:T(8,128)}), (f32[8,64,128]{2,1,0:T(8,128)}, f32[8,64,64]{1,2,0:T(8,128)})) %all-reduce.3.cloned.1.call-update) | async-done | bytes 393232 | tf_op jit(solution)/shard_map/psum | solution.py:48
  402.8 1.5 multiply_reduce_fusion
  404.3 0.2 bitcast_multiply_fusion
  404.6 9.3 %all-gather = f32[8,4,2048]{2,1,0:T(4,128)S(1)} all-gather(f32[1,4,2048]{2,1,0:T(4,128)S(1)} %dynamic-slice_bitcast_fusion), channel_id=1, replica_groups=mesh['dp'=2,'tensor'=4,'fsdp'=4] {'dp','fsdp'}, dimensions={0}, use_global_device_ids=true | all-gather | bytes 294912 | tf_op jit(solution)/shard_map/all_gather | solution.py:62
  413.8 0.1 reshape.41
  413.9 0.3 fusion.8
  414.2 10.6 %psum.23 = f32[4,32]{1,0:T(4,128)S(1)} all-reduce(f32[4,32]{1,0:T(4,128)S(1)} %fusion.8), channel_id=1, replica_groups=mesh['dp'=2,'tensor'=4,'fsdp'=4] {'tensor'}, use_global_device_ids=true, to_apply=%region_3.4 | all-reduce | flops 128 | bytes 1024 | tf_op jit(solution)/shard_map/psum | solution.py:69
  424.8 0.6 broadcast_multiply_fusion
  (22 shorter events, 0.4 us)
Async XLA Ops:
  6.5 336.5 %copy-start = (bf16[2752,64]{0,1:T(8,128)(2,1)S(1)}, bf16[2752,64]{0,1:T(8,128)(2,1)}, u32[]{:S(2)}) copy-start(bf16[2752,64]{0,1:T(8,128)(2,1)} %param.18) | copy-start | bytes 1056772
  6.5 2.8 copy-start.2
  6.5 2.9 copy-start.1
  6.5 2.9 copy-start.3
  6.5 50.8 %all-gather.6.cloned.1.call-start = ((), (), s32[]{:S(2)}) async-start(), calls=%async_computation | async-start | bytes 2621440 | tf_op jit(solution)/shard_map/all_gather | solution.py:28
  7.3 96.1 %all-gather.8.cloned.1.call-start = ((), (), s32[]{:S(2)}) async-start(), calls=%async_computation.1 | async-start | bytes 2621440 | tf_op jit(solution)/shard_map/all_gather | solution.py:29
  8.0 214.7 %all-gather.10.cloned.1.call-start = ((), (), s32[]{:S(2)}) async-start(), calls=%async_computation.2 | async-start | bytes 25362432 | tf_op jit(solution)/shard_map/all_gather | solution.py:35
  8.8 334.3 %all-gather.12.cloned.1.call-start = ((), (), s32[]{:S(2)}) async-start(), calls=%async_computation.3 | async-start | bytes 25362432 | tf_op jit(solution)/shard_map/all_gather | solution.py:40
  9.3 393.4 %all-reduce.3.cloned.1.call-start = ((), (), s32[]{:S(2)}) async-start(), calls=%async_computation.4 | async-start | bytes 1048576 | tf_op jit(solution)/shard_map/psum | solution.py:48
  241.9 122.1 %copy-start.4 = (s32[4]{0:T(128)S(1)}, s32[4]{0:T(128)}, u32[]{:S(2)}) copy-start(s32[4]{0:T(128)} %param.15) | copy-start | bytes 52
  241.9 122.1 %copy-start.5 = (s32[4]{0:T(128)S(1)}, s32[4]{0:T(128)}, u32[]{:S(2)}) copy-start(s32[4]{0:T(128)} %param.14) | copy-start | bytes 52
Sparse Core Ops, SparseCore 0:
  8.9 48.3 all-gather.5
  58.9 44.4 all-gather.7
  105.3 117.3 all-gather.9
  224.4 118.5 all-gather.11
  364.1 38.6 all-reduce.2
where the time goes:
time: 432 us
  waiting for transfers between devices  348 us (81%)
  matrix products  42.2 us (10%)
  blocking collectives  19.9 us (5%)
  between operations  13.2 us (3%)
  local copies, waits for them, and re-layouts  7.28 us (2%)
    all_gather x1, waiting for transfers between devices, on_device(): lax.all_gather(gate_weight, ('dp', 'fsdp'), axis=0, tiled=True)  116 us
    all_gather x1, waiting for transfers between devices, on_device(): lax.all_gather(up_weight, ('dp', 'fsdp'), axis=0, tiled=True)  101 us
    all_gather x1, waiting for transfers between devices, on_device(): lax.all_gather(train_acts, 'tensor', axis=1, tiled=True)  46.8 us
    all_gather x1, waiting for transfers between devices, on_device(): lax.all_gather(val_acts, 'tensor', axis=1, tiled=True)  42.9 us
    psum x1, waiting for transfers between devices, on_device(): in_proj, out_proj = lax.psum((in_part, out_part), 'tensor')  38.7 us
    dot_general x1, matrix products, on_device(): in_part = jnp.dot(hidden, in_basis, preferred_element_type=jnp.float32)  20 us
    dot_general x1, matrix products, on_device(): jnp.dot(activations, lax.all_gather(gate_weight, ('dp', 'fsdp'), axis=0,...  19.2 us
    psum x1, blocking collectives, on_device(): product = lax.psum(partial_scores, 'tensor')  10.6 us
  transfers between devices with their start and end apart: 5, of which 5 were waited for; matrix products, arithmetic and copies ran while one was open for 6% of the time, Pallas kernels for 0%

commit v1 on v0

--- a/solution.py
+++ b/solution.py
@@ -4,6 +4,23 @@
 from jax.sharding import PartitionSpec as P
 
 SEQ = 64
+
+
+def joined_along(parts, dim):
+    parts = jnp.moveaxis(parts, 0, dim)
+    dims = parts.shape
+    return parts.reshape(*dims[:dim], dims[dim] * dims[dim + 1], *dims[dim + 2 :])
+
+
+def ring_gather(x, axis, dim):
+    size = lax.axis_size(axis)
+    forward = [(i, (i + 1) % size) for i in range(size)]
+    blocks = [x]
+    while len(blocks) < size:
+        blocks.append(lax.ppermute(blocks[-1], axis, forward))
+    here = lax.axis_index(axis)
+    blocks = jnp.stack(blocks)[(here - jnp.arange(size)) % size]
+    return joined_along(blocks, dim)
 
 
 def outer_sums(in_proj, out_proj, valid):
@@ -36,9 +53,7 @@
         preferred_element_type=jnp.float32,
     )
     up_sum = jnp.dot(
-        activations,
-        lax.all_gather(up_weight, ("dp", "fsdp"), axis=0, tiled=True),
-        preferred_element_type=jnp.float32,
+        activations, ring_gather(up_weight, ("dp", "fsdp"), 0), preferred_element_type=jnp.float32
     )
     hidden = (jax.nn.silu(gate_sum) * up_sum).astype(jnp.bfloat16)
     in_part = jnp.dot(hidden, in_basis, preferred_element_type=jnp.float32)

time: 432 us -> 540 us (1.25)
  local copies, waits for them, and re-layouts: 7.28 us -> 101 us
  other arithmetic: 0.9 us -> 24.3 us
  waiting for transfers between devices: 348 us -> 336 us
    ppermute x0 -> x7, waiting for transfers between devices: none -> 294 us  [ring_gather(): blocks.append(lax.ppermute(blocks[-1], axis, forward))]
    all_gather x1, waiting for transfers between devices: 116 us -> 0.01 us  [on_device(): lax.all_gather(gate_weight, ('dp', 'fsdp'), axis=0, tiled=True)]
    all_gather x1 -> x0, waiting for transfers between devices: 101 us -> none  [on_device(): lax.all_gather(up_weight, ('dp', 'fsdp'), axis=0, tiled=True)]
    unnamed x15 -> x21, local copies, waits for them, and re-layouts: 3.24 us -> 55.1 us
    all_gather x1, waiting for transfers between devices: 46.8 us -> 0.01 us  [on_device(): lax.all_gather(train_acts, 'tensor', axis=1, tiled=True)]
    all_gather x1, waiting for transfers between devices: 42.9 us -> 0.01 us  [on_device(): lax.all_gather(val_acts, 'tensor', axis=1, tiled=True)]
    gather x0 -> x4, local copies, waits for them, and re-layouts: none -> 40.2 us  [ring_gather(): blocks = jnp.stack(blocks)[(here - jnp.arange(size)) % size]]
    unnamed x0 -> x1, other arithmetic: none -> 23.4 us
  transfers between devices with their start and end apart: 5 -> 11, of which waited for: 5 -> 8; matrix products, arithmetic and copies ran while one was open for 6% -> 23% of each run, Pallas kernels for 0% -> 0%
where the time goes in v1:
time: 540 us; the launch traced here: 539 us
  waiting for transfers between devices  336 us (62%)
  local copies, waits for them, and re-layouts  101 us (19%)
  matrix products  43.6 us (8%)
  other arithmetic  24.3 us (4%)
  blocking collectives  19.9 us (4%)
  between operations  13.2 us (2%)
    ppermute x7, waiting for transfers between devices, ring_gather(): blocks.append(lax.ppermute(blocks[-1], axis, forward))  294 us
    unnamed x21, local copies, waits for them, and re-layouts  55.1 us
    gather x4, local copies, waits for them, and re-layouts, ring_gather(): blocks = jnp.stack(blocks)[(here - jnp.arange(size)) % size]  40.2 us
    psum x1, waiting for transfers between devices, on_device(): in_proj, out_proj = lax.psum((in_part, out_part), 'tensor')  39.4 us
    unnamed x1, other arithmetic  23.4 us
    dot_general x1, matrix products, on_device(): in_part = jnp.dot(hidden, in_basis, preferred_element_type=jnp.float32)  20.3 us
    dot_general x1, matrix products, on_device(): jnp.dot(activations, lax.all_gather(gate_weight, ('dp', 'fsdp'), axis=0,...  19 us
  transfers between devices with their start and end apart: 11, of which 8 were waited for; matrix products, arithmetic and copies ran while one was open for 23% of the time, Pallas kernels for 0%

profile of v1, /device:TPU:0, one launch (start us, length us, event | category | flops | bytes accessed | tf_op | source)
XLA Modules:
  0.0 538.7 jit_solution(12873274405071455922)
XLA Ops:
  9.3 34.5 %collective-permute-done = bf16[512,2752]{0,1:T(8,128)(2,1)S(1)} collective-permute-done((bf16[512,2752]{0,1:T(8,128)(2,1)}, bf16[512,2752]{0,1:T(8,128)(2,1)S(1)}, u32[]{:S(2)}, u32[]{:S(2)}) %collective-permute-start) | collective-permute-done | bytes 2818080 | tf_op jit(solution)/shard_map/ppermute | solution.py:20
  43.9 34.1 %collective-permute-done.1 = bf16[512,2752]{0,1:T(8,128)(2,1)S(1)} collective-permute-done((bf16[512,2752]{0,1:T(8,128)(2,1)S(1)}, bf16[512,2752]{0,1:T(8,128)(2,1)S(1)}, u32[]{:S(2)}, u32[]{:S(2)}) %collective-permute-start.1) | collective-permute-done | bytes 2818080 | tf_op jit(solution)/shard_map/ppermute | solution.py:20
  77.9 34.1 %collective-permute-done.2 = bf16[512,2752]{0,1:T(8,128)(2,1)S(1)} collective-permute-done((bf16[512,2752]{0,1:T(8,128)(2,1)S(1)}, bf16[512,2752]{0,1:T(8,128)(2,1)S(1)}, u32[]{:S(2)}, u32[]{:S(2)}) %collective-permute-start.2) | collective-permute-done | bytes 2818080 | tf_op jit(solution)/shard_map/ppermute | solution.py:20
  112.0 64.4 %collective-permute-done.3 = bf16[512,2752]{0,1:T(8,128)(2,1)} collective-permute-done((bf16[512,2752]{0,1:T(8,128)(2,1)S(1)}, bf16[512,2752]{0,1:T(8,128)(2,1)}, u32[]{:S(2)}, u32[]{:S(2)}) %collective-permute-start.3) | collective-permute-done | bytes 2818080 | tf_op jit(solution)/shard_map/ppermute | solution.py:20
  178.9 3.5 bitcast_dynamic-update-slice_fusion.7
  182.4 78.0 %collective-permute-done.4 = bf16[512,2752]{0,1:T(8,128)(2,1)} collective-permute-done((bf16[512,2752]{0,1:T(8,128)(2,1)}, bf16[512,2752]{0,1:T(8,128)(2,1)}, u32[]{:S(2)}, u32[]{:S(2)}) %collective-permute-start.4) | collective-permute-done | bytes 2818080 | tf_op jit(solution)/shard_map/ppermute | solution.py:20
  260.5 3.5 bitcast_dynamic-update-slice_fusion.6
  270.3 3.6 bitcast_dynamic-update-slice_fusion.5
  273.9 27.5 %collective-permute-done.5 = bf16[512,2752]{0,1:T(8,128)(2,1)} collective-permute-done((bf16[512,2752]{0,1:T(8,128)(2,1)}, bf16[512,2752]{0,1:T(8,128)(2,1)}, u32[]{:S(2)}, u32[]{:S(2)}) %collective-permute-start.5) | collective-permute-done | bytes 2818080 | tf_op jit(solution)/shard_map/ppermute | solution.py:20
  303.2 3.6 bitcast_dynamic-update-slice_fusion.3
  306.8 3.5 bitcast_dynamic-update-slice_fusion.2
  310.3 3.5 bitcast_dynamic-update-slice_fusion.1
  313.9 21.8 %collective-permute-done.6 = bf16[512,2752]{0,1:T(8,128)(2,1)S(1)} collective-permute-done((bf16[512,2752]{0,1:T(8,128)(2,1)}, bf16[512,2752]{0,1:T(8,128)(2,1)S(1)}, u32[]{:S(2)}, u32[]{:S(2)}) %collective-permute-start.6) | collective-permute-done | bytes 2818080 | tf_op jit(solution)/shard_map/ppermute | solution.py:20
  337.5 9.8 %mini-gather-slice.2 = bf16[8,512,1408]{1,2,0:T(8,128)(2,1)} slice(bf16[8,512,2752]{1,2,0:T(8,128)(2,1)} %bitcast_dynamic-update-slice_fusion), slice={[0:8], [0:512], [0:1408]} | slice | bytes 23068672 | tf_op jit(solution)/shard_map/gather | solution.py:22
  347.3 10.1 %mini-gather-slice.3 = bf16[8,512,1344]{1,2,0:T(8,128)(2,1)} slice(bf16[8,512,2752]{1,2,0:T(8,128)(2,1)} %bitcast_dynamic-update-slice_fusion), slice={[0:8], [0:512], [1408:2752]} | slice | bytes 22020096 | tf_op jit(solution)/shard_map/gather | solution.py:22
  357.4 10.4 %gather_fusion = bf16[8,512,1408]{1,2,0:T(8,128)(2,1)} fusion(bf16[8,512,1408]{1,2,0:T(8,128)(2,1)} %mini-gather-slice.2, s32[1024]{0:T(1024)S(1)} %pad_clamp_fusion), kind=kCustom, calls=%fused_computation | custom fusion | bytes 23068704 | tf_op jit(solution)/shard_map/gather | solution.py:22
  367.7 9.9 %gather_fusion.1 = bf16[8,512,1344]{1,2,0:T(8,128)(2,1)} fusion(bf16[8,512,1344]{1,2,0:T(8,128)(2,1)} %mini-gather-slice.3, s32[1024]{0:T(1024)S(1)} %pad_clamp_fusion), kind=kCustom, calls=%fused_computation.1 | custom fusion | bytes 22020128 | tf_op jit(solution)/shard_map/gather | solution.py:22
  377.6 23.4 %pad_maximum_fusion = bf16[8,512,2752]{1,2,0:T(8,128)(2,1)} fusion(bf16[8,512,1344]{1,2,0:T(8,128)(2,1)} %gather_fusion.1, bf16[8,512,1408]{1,2,0:T(8,128)(2,1)} %gather_fusion), kind=kLoop, calls=%fused_computation.2 | loop fusion | flops 45088768 | bytes 45088768
  401.0 28.7 %copy.14 = bf16[8,512,2752]{2,1,0:T(8,128)(2,1)} copy(bf16[8,512,2752]{1,2,0:T(8,128)(2,1)} %pad_maximum_fusion) | data formatting | bytes 45088768
  429.7 19.0 %fusion.15 = f32[512,2752]{0,1:T(8,128)} fusion(bf16[512,4096]{1,0:T(8,128)(2,1)} %constant_dynamic-update-slice_fusion, bf16[4096,2752]{0,1:T(8,128)(2,1)} %all-gather.9.cloned.1.call-done), kind=kOutput, calls=%fused_computation.41 | convolution fusion | flops 11542724608 | bytes 32374784 | tf_op jit(solution)/shard_map/dot_general | solution.py:50
  448.7 20.3 %fusion.16 = f32[512,64]{0,1:T(8,128)S(1)} fusion(bf16[2752,64]{0,1:T(8,128)(2,1)S(1)} %copy-done, f32[512,2752]{0,1:T(8,128)} %fusion.15, bf16[512,4096]{1,0:T(8,128)(2,1)} %constant_dynamic-update-slice_fusion, bf16[4096,2752]{1,0:T(8,128)(2,1)} %bitcast.44), kind=kOutput, calls=%fused_computation.42 | convolution fusion | flops 11731533824 | bytes 32858112 | tf_op jit(solution)/shard_map/dot_general | solution.py:59
  470.1 39.4 %all-reduce.3.cloned.1.call-done = (f32[8,64,128]{2,1,0:T(8,128)}, f32[8,64,64]{1,2,0:T(8,128)}) async-done(((f32[8,64,128]{2,1,0:T(8,128)}, f32[8,64,64]{1,2,0:T(8,128)}), (f32[8,64,128]{2,1,0:T(8,128)}, f32[8,64,64]{1,2,0:T(8,128)})) %all-reduce.3.cloned.1.call-update) | async-done | bytes 393232 | tf_op jit(solution)/shard_map/psum | solution.py:63
  511.3 9.3 %all-gather = f32[8,4,2048]{2,1,0:T(4,128)S(1)} all-gather(f32[1,4,2048]{2,1,0:T(4,128)S(1)} %dynamic-slice_bitcast_fusion), channel_id=1, replica_groups=mesh['dp'=2,'tensor'=4,'fsdp'=4] {'dp','fsdp'}, dimensions={0}, use_global_device_ids=true | all-gather | bytes 294912 | tf_op jit(solution)/shard_map/all_gather | solution.py:77
  520.9 10.6 %psum.23 = f32[4,32]{1,0:T(4,128)S(1)} all-reduce(f32[4,32]{1,0:T(4,128)S(1)} %fusion.7), channel_id=1, replica_groups=mesh['dp'=2,'tensor'=4,'fsdp'=4] {'tensor'}, use_global_device_ids=true, to_apply=%region_3.4 | all-reduce | flops 128 | bytes 1024 | tf_op jit(solution)/shard_map/psum | solution.py:84
  (47 shorter events, 18.9 us)
Async XLA Ops:
  6.5 442.2 %copy-start = (bf16[2752,64]{0,1:T(8,128)(2,1)S(1)}, bf16[2752,64]{0,1:T(8,128)(2,1)}, u32[]{:S(2)}) copy-start(bf16[2752,64]{0,1:T(8,128)(2,1)} %param.18) | copy-start | bytes 1056772
  6.5 257.5 %all-gather.5.cloned.1.call-start = ((), (), s32[]{:S(2)}) async-start(), calls=%async_computation | async-start | bytes 2621440 | tf_op jit(solution)/shard_map/all_gather | solution.py:45
  7.3 259.9 %all-gather.7.cloned.1.call-start = ((), (), s32[]{:S(2)}) async-start(), calls=%async_computation.1 | async-start | bytes 2621440 | tf_op jit(solution)/shard_map/all_gather | solution.py:46
  8.0 421.7 %all-gather.9.cloned.1.call-start = ((), (), s32[]{:S(2)}) async-start(), calls=%async_computation.2 | async-start | bytes 25362432 | tf_op jit(solution)/shard_map/all_gather | solution.py:52
  8.7 500.8 %all-reduce.3.cloned.1.call-start = ((), (), s32[]{:S(2)}) async-start(), calls=%async_computation.3 | async-start | bytes 1048576 | tf_op jit(solution)/shard_map/psum | solution.py:63
  8.8 35.1 %collective-permute-start = (bf16[512,2752]{0,1:T(8,128)(2,1)}, bf16[512,2752]{0,1:T(8,128)(2,1)S(1)}, u32[]{:S(2)}, u32[]{:S(2)}) collective-permute-start(bf16[512,2752]{0,1:T(8,128)(2,1)} %param.17), channel_id=1, source_target_pairs={{0,1},{1,2},{2,3},{3,16},{16,17},{17,18},{18,19},{19,0},{4,5},{5,6... | collective-permute-start | bytes 8454152 | tf_op jit(solution)/shard_map/ppermute | solution.py:20
  43.9 132.6 %copy-start.2 = (bf16[512,2752]{0,1:T(8,128)(2,1)}, bf16[512,2752]{0,1:T(8,128)(2,1)S(1)}, u32[]{:S(2)}) copy-start(bf16[512,2752]{0,1:T(8,128)(2,1)S(1)} %collective-permute-done) | copy-start | bytes 8454148
  43.9 34.1 %collective-permute-start.1 = (bf16[512,2752]{0,1:T(8,128)(2,1)S(1)}, bf16[512,2752]{0,1:T(8,128)(2,1)S(1)}, u32[]{:S(2)}, u32[]{:S(2)}) collective-permute-start(bf16[512,2752]{0,1:T(8,128)(2,1)S(1)} %collective-permute-done), channel_id=1, source_target_pairs={{0,1},{1,2},{2,3},{3,16},{16,17},{17,18},{18,19},{19,0},{4,5},{5,6... | collective-permute-start | bytes 8454152 | tf_op jit(solution)/shard_map/ppermute | solution.py:20
  77.9 98.5 %copy-start.1 = (bf16[512,2752]{0,1:T(8,128)(2,1)}, bf16[512,2752]{0,1:T(8,128)(2,1)S(1)}, u32[]{:S(2)}) copy-start(bf16[512,2752]{0,1:T(8,128)(2,1)S(1)} %collective-permute-done.1) | copy-start | bytes 8454148
  77.9 34.1 %collective-permute-start.2 = (bf16[512,2752]{0,1:T(8,128)(2,1)S(1)}, bf16[512,2752]{0,1:T(8,128)(2,1)S(1)}, u32[]{:S(2)}, u32[]{:S(2)}) collective-permute-start(bf16[512,2752]{0,1:T(8,128)(2,1)S(1)} %collective-permute-done.1), channel_id=1, source_target_pairs={{0,1},{1,2},{2,3},{3,16},{16,17},{17,18},{18,19},{19,0},{4,5},{5,6... | collective-permute-start | bytes 8454152 | tf_op jit(solution)/shard_map/ppermute | solution.py:20
  112.0 64.4 %collective-permute-start.3 = (bf16[512,2752]{0,1:T(8,128)(2,1)S(1)}, bf16[512,2752]{0,1:T(8,128)(2,1)}, u32[]{:S(2)}, u32[]{:S(2)}) collective-permute-start(bf16[512,2752]{0,1:T(8,128)(2,1)S(1)} %collective-permute-done.2), channel_id=1, source_target_pairs={{0,1},{1,2},{2,3},{3,16},{16,17},{17,18},{18,19},{19,0},{4,5},{5,6... | collective-permute-start | bytes 8454152 | tf_op jit(solution)/shard_map/ppermute | solution.py:20
  176.4 84.0 %collective-permute-start.4 = (bf16[512,2752]{0,1:T(8,128)(2,1)}, bf16[512,2752]{0,1:T(8,128)(2,1)}, u32[]{:S(2)}, u32[]{:S(2)}) collective-permute-start(bf16[512,2752]{0,1:T(8,128)(2,1)} %collective-permute-done.3), channel_id=1, source_target_pairs={{0,1},{1,2},{2,3},{3,16},{16,17},{17,18},{18,19},{19,0},{4,5},{5,6... | collective-permute-start | bytes 8454152 | tf_op jit(solution)/shard_map/ppermute | solution.py:20
  260.4 41.0 %collective-permute-start.5 = (bf16[512,2752]{0,1:T(8,128)(2,1)}, bf16[512,2752]{0,1:T(8,128)(2,1)}, u32[]{:S(2)}, u32[]{:S(2)}) collective-permute-start(bf16[512,2752]{0,1:T(8,128)(2,1)} %collective-permute-done.4), channel_id=1, source_target_pairs={{0,1},{1,2},{2,3},{3,16},{16,17},{17,18},{18,19},{19,0},{4,5},{5,6... | collective-permute-start | bytes 8454152 | tf_op jit(solution)/shard_map/ppermute | solution.py:20
  301.4 34.3 %collective-permute-start.6 = (bf16[512,2752]{0,1:T(8,128)(2,1)}, bf16[512,2752]{0,1:T(8,128)(2,1)S(1)}, u32[]{:S(2)}, u32[]{:S(2)}) collective-permute-start(bf16[512,2752]{0,1:T(8,128)(2,1)} %collective-permute-done.5), channel_id=1, source_target_pairs={{0,1},{1,2},{2,3},{3,16},{16,17},{17,18},{18,19},{19,0},{4,5},{5,6... | collective-permute-start | bytes 8454152 | tf_op jit(solution)/shard_map/ppermute | solution.py:20
  448.7 21.2 %copy-start.3 = (s32[4]{0:T(128)S(1)}, s32[4]{0:T(128)}, u32[]{:S(2)}) copy-start(s32[4]{0:T(128)} %param.15) | copy-start | bytes 52
  448.7 21.2 %copy-start.4 = (s32[4]{0:T(128)S(1)}, s32[4]{0:T(128)}, u32[]{:S(2)}) copy-start(s32[4]{0:T(128)} %param.14) | copy-start | bytes 52
Sparse Core Ops, SparseCore 0:
  8.9 48.3 all-gather.4
  58.9 44.4 all-gather.6
  105.3 176.5 all-gather.8
  470.0 39.4 all-reduce.2
